TPU v7x, 128 devices: a whole 4x4x4 slice. The times are simulated.
128 devices in a mesh: wide: 16 (over z_lo, x, core), narrow: 8 (over z_hi, y).
Axes of the slice: x: 4, y: 4, z: 4 (z_hi: 2, z_lo: 2; z = z_hi * 2 + z_lo), core: 2. Of those that a mesh axis runs over, the one named last changes fastest.
Arguments:
- vectors: float32 [32000, 8192], P('wide', 'narrow'), may hold values from -0.44860464 to 0.44860464
- reflectors: float32 [32000, 256], P('wide'), may hold values from -6 to 6
- triangle: float32 [256, 256], replicated, may hold values from -3.125e-05 to 7.8125e-05, as said below
- energies: float32 [32000], P('wide'), may hold values from -1 to 1
Outputs:
- updated: float32 [32000, 8192], P('wide', 'narrow')
- fock_block: float32 [8192, 512], P(('narrow', 'wide'))
Inputs may be any that keep to these rules, and one draw needn't show every extreme that they name: `triangle`: upper triangular, with diagonal entries between 1.5 / 32000 and 2.5 / 32000 and entries above the diagonal of magnitude at most 1 / 32000.
All inputs are finite; a program needn't handle non-finite values.
Results may differ from a plain program's by a relative error of at most 0.00007.
Values sent between devices are 32-bit elements; how exact they have to be, the bound alone decides.
A program may use at most 64 MiB of HBM per device.

v0:
```python
import jax
import jax.numpy as jnp
from jax import lax
from jax.sharding import PartitionSpec as P

FB = 512
OFF = 256


def on_device(vectors, reflectors, triangle, energies):
    highest = lax.Precision.HIGHEST
    contract_rows = (((0,), (0,)), ((), ()))
    partial_proj = lax.dot_general(
        reflectors, vectors, contract_rows, precision=highest, preferred_element_type=jnp.float32
    )
    projected = lax.psum(partial_proj, "wide")
    coefficients = jnp.dot(
        triangle, projected, precision=highest, preferred_element_type=jnp.float32
    )
    updated = vectors - jnp.dot(
        reflectors, coefficients, precision=highest, preferred_element_type=jnp.float32
    )
    block_width = FB // lax.axis_size("narrow")
    scaled_rows = energies[:, None]
    own_columns = updated[:, OFF : OFF + block_width]
    fock_part = lax.dot_general(
        updated,
        scaled_rows * lax.all_gather(own_columns, "narrow", axis=1, tiled=True),
        contract_rows,
        precision=highest,
        preferred_element_type=jnp.float32,
    )
    fock_block = lax.psum_scatter(fock_part, "wide", scatter_dimension=0, tiled=True)
    return (updated, fock_block)


def solution(mesh):
    return jax.shard_map(
        on_device,
        mesh=mesh,
        in_specs=(P("wide", "narrow"), P("wide", None), P(), P("wide")),
        out_specs=(P("wide", "narrow"), P(("narrow", "wide"), None)),
        check_vma=False,
    )
```

profile of v0, /device:TPU:1, one launch (start us, length us, event | category | flops | bytes accessed | tf_op | source)
XLA Modules:
  0.0 328.7 jit_solution(17670768227065324609)
XLA Ops:
  7.2 0.0 copy-start
  7.2 0.0 copy-start.2
  7.2 0.0 all-reduce.2.cloned.1.call-start
  7.2 1.5 copy-done
  8.7 10.3 %fusion.3 = f32[256,1024]{1,0:T(8,128)} fusion(f32[2000,256]{1,0:T(8,128)S(1)} %copy-done, f32[2000,1024]{1,0:T(8,128)} %param.4), kind=kOutput, calls=%fused_computation.4 | convolution fusion | flops 6291456000 | bytes 11288576 | tf_op jit(solution)/shard_map/dot_general | solution.py:13
  19.1 0.0 all-reduce.2.cloned.1.call-update
  19.1 0.0 all-gather.2.cloned.1.call-start
  19.1 123.5 %all-reduce.2.cloned.1.call-done = f32[256,1024]{1,0:T(8,128)} async-done(((f32[256,1024]{1,0:T(8,128)}), f32[256,1024]{1,0:T(8,128)}) %all-reduce.2.cloned.1.call-update) | async-done | bytes 1048592 | tf_op jit(solution)/shard_map/psum | solution.py:16
  142.6 0.0 copy-done.2
  142.6 3.0 fusion.4
  145.7 0.0 copy-start.3
  145.7 9.6 %bitcast_subtract_fusion = f32[2000,1024]{1,0:T(8,128)S(1)} fusion(f32[2000,1024]{1,0:T(8,128)} %param.4, f32[1024,256]{1,0:T(8,128)S(1)} %fusion.4, f32[2000,256]{1,0:T(8,128)S(1)} %copy-done), kind=kOutput, calls=%fused_computation | convolution fusion | flops 6293504000 | bytes 19480576 | tf_op jit(solution)/shard_map/dot_general | solution.py:20
  155.3 0.0 copy-start.1
  155.3 3.3 %copy-done.1 = f32[2000,1024]{1,0:T(8,128)} copy-done((f32[2000,1024]{1,0:T(8,128)}, f32[2000,1024]{1,0:T(8,128)S(1)}, u32[]{:S(2)}) %copy-start.1) | copy-done | bytes 8192024
  158.6 0.1 slice.4
  158.8 1.1 copy.6
  159.9 0.0 all-gather.2.cloned.1.call-update
  159.9 0.0 reduce-scatter.2.cloned.1.call-start
  160.0 72.3 %all-gather.2.cloned.1.call-done = f32[2000,512]{0,1:T(8,128)} async-done(((f32[2000,64]{0,1:T(8,128)}), f32[2000,512]{0,1:T(8,128)}) %all-gather.2.cloned.1.call-update) | async-done | bytes 4096016 | tf_op jit(solution)/shard_map/all_gather | solution.py:28
  232.2 0.0 copy-done.3
  232.2 30.9 %fusion = f32[1024,512]{1,0:T(8,128)} fusion(f32[2000,1024]{1,0:T(8,128)} %copy-done.1, f32[2000,512]{0,1:T(8,128)} %all-gather.2.cloned.1.call-done, f32[2000]{0:T(1024)S(1)} %copy-done.3), kind=kOutput, calls=%fused_computation.1 | convolution fusion | flops 12583936000 | bytes 14393152 | tf_op jit(solution)/shard_map/dot_general | solution.py:26
  263.1 0.0 reduce-scatter.2.cloned.1.call-update
  263.2 59.0 %reduce-scatter.2.cloned.1.call-done = f32[64,512]{1,0:T(8,128)} async-done(((f32[1024,512]{1,0:T(8,128)}), f32[64,512]{1,0:T(8,128)}) %reduce-scatter.2.cloned.1.call-update) | async-done | bytes 131088 | tf_op jit(solution)/shard_map/reduce_scatter | solution.py:33
Async XLA Ops:
  7.2 1.6 copy-start
  7.2 135.4 %copy-start.2 = (f32[256,256]{1,0:T(8,128)S(1)}, f32[256,256]{1,0:T(8,128)}, u32[]{:S(2)}) copy-start(f32[256,256]{1,0:T(8,128)} %param.6) | copy-start | bytes 786436
  7.2 135.4 %all-reduce.2.cloned.1.call-start = ((), (), s32[]{:S(2)}) async-start(), calls=%async_computation.1 | async-start | bytes 2097152 | tf_op jit(solution)/shard_map/psum | solution.py:16
  19.1 213.2 %all-gather.2.cloned.1.call-start = ((), (), s32[]{:S(2)}) async-start(), calls=%async_computation.2 | async-start | bytes 4718592 | tf_op jit(solution)/shard_map/all_gather | solution.py:28
  145.7 86.6 %copy-start.3 = (f32[2000]{0:T(1024)S(1)}, f32[2000]{0:T(1024)}, u32[]{:S(2)}) copy-start(f32[2000]{0:T(1024)} %param.7) | copy-start | bytes 24004
  155.3 3.3 %copy-start.1 = (f32[2000,1024]{1,0:T(8,128)}, f32[2000,1024]{1,0:T(8,128)S(1)}, u32[]{:S(2)}) copy-start(f32[2000,1024]{1,0:T(8,128)S(1)} %bitcast_subtract_fusion) | copy-start | bytes 24576004
  159.9 162.2 %reduce-scatter.2.cloned.1.call-start = ((), (), s32[]{:S(2)}) async-start(), calls=%async_computation.3 | async-start | bytes 2228224 | tf_op jit(solution)/shard_map/reduce_scatter | solution.py:33
Sparse Core Ops, SparseCore 0:
  19.2 123.3 all-reduce.1
  160.0 72.1 all-gather.1
  263.3 58.8 reduce-scatter.1
where the time goes:
time: 332 us; the launch traced here: 329 us
  waiting for transfers between devices  255 us (77%)
  matrix products  53.8 us (16%)
  between operations  13.8 us (4%)
  local copies, waits for them, and re-layouts  6.11 us (2%)
    psum x1, waiting for transfers between devices, on_device(): projected = lax.psum(partial_proj, 'wide')  123 us
    all_gather x1, waiting for transfers between devices, on_device(): lax.all_gather(own_columns, 'narrow', axis=1, tiled=True)  72.3 us
    reduce_scatter x1, waiting for transfers between devices, on_device(): lax.psum_scatter(fock_part, 'wide', scatter_dimension=0, tiled=True)  59 us
    dot_general x1, matrix products, on_device(): lax.dot_general(updated, scaled_rows * lax.all_gather(own_columns, 'narro...  30.9 us
    dot_general x1, matrix products, on_device(): lax.dot_general(reflectors, vectors, contract_rows, precision=highest, pr...  10.3 us
    dot_general x1, matrix products, on_device(): jnp.dot(reflectors, coefficients, precision=highest, preferred_element_ty...  9.61 us
  transfers between devices with their start and end apart: 3, of which 3 were waited for; matrix products, arithmetic and copies ran while one was open for 0% of the time, Pallas kernels for 0%

commit v1 on v0

v1 whole, which is shorter than its diff:
```python
import functools

import jax
import jax.numpy as jnp
from jax import lax
from jax.experimental import pallas as pl
from jax.experimental.pallas import tpu as pltpu
from jax.sharding import PartitionSpec as P

MESH = pl.DeviceIdType.MESH
F32, BF16 = jnp.float32, jnp.bfloat16
ROWS, KP, NC, NB = 2000, 2048, 1024, 256
FB, OFF, BW = 512, 256, 64


def dot(a, b):
    return jnp.dot(a, b, preferred_element_type=F32)


def split(x):
    hi = x.astype(BF16)
    return hi, (x - hi.astype(F32)).astype(BF16)


def dot3(a, b):
    return dot(a[0], b[0]) + dot(a[0], b[1]) + dot(a[1], b[0])


def mult(i, m):
    return pl.multiple_of(i * m, m)


def kernel(
    v_hbm, r_hbm, t_ref, e_ref, u_hbm, f_ref,
    v, r, vb, rtr, rt, rtt, uu, vbt, pbt, ep, part, xrecv, rsr, pred, pfull, ub, red, fo, fsend,
    ld_sem, out_sem, ag_s, ag_r, xs, xr, rs_s, rs_r, pa_s, pa_r, pr_s, pr_r, pb_s, pb_r, f_s, f_r,
):
    w, n = lax.axis_index("wide"), lax.axis_index("narrow")
    c, k = lax.rem(w, 2), w // 2
    y, zh = lax.rem(n, 4), n // 4
    partner = (w + 1 - 2 * c, n)
    yp, ym = zh * 4 + lax.rem(y + 1, 4), zh * 4 + lax.rem(y + 3, 4)
    base = zh * 4
    zbase = (1 - zh) * 4

    def same_core(kk):
        return (2 * kk + c, n)

    def narrow_peer(nn):
        return (w, nn)

    def remote(src, dst, s, rsem, to):
        return pltpu.make_async_remote_copy(
            src_ref=src, dst_ref=dst, send_sem=s, recv_sem=rsem, device_id=to, device_id_type=MESH
        )

    kk0 = k // 2

    def order(s):
        return lax.rem(kk0 + 1 + s, 4)

    vb_load = pltpu.make_async_copy(v_hbm.at[:, pl.ds(OFF, 128)], vb.at[pl.ds(0, ROWS)], ld_sem.at[0])
    r_load = pltpu.make_async_copy(r_hbm, r.at[pl.ds(0, ROWS)], ld_sem.at[1])

    def v_load(i):
        cols = pl.ds(mult(i, 256), 256)
        return pltpu.make_async_copy(v_hbm.at[:, cols], v.at[pl.ds(0, ROWS), cols], ld_sem.at[2 + i])

    vb_load.start()
    r_load.start()
    for s in range(4):
        v_load(order(s)).start()

    barrier = pltpu.get_barrier_semaphore()
    pl.semaphore_signal(barrier, inc=1, device_id=partner, device_id_type=MESH)
    for d in range(1, 8):
        pl.semaphore_signal(barrier, inc=1, device_id=same_core(lax.rem(k + d, 8)), device_id_type=MESH)
        pl.semaphore_signal(barrier, inc=1, device_id=narrow_peer(lax.rem(n + d, 8)), device_id_type=MESH)

    vb[ROWS:, :] = jnp.zeros((KP - ROWS, 128), F32)
    r[ROWS:, :] = jnp.zeros((KP - ROWS, NB), F32)
    v[ROWS:, :] = jnp.zeros((KP - ROWS, NC), F32)
    ep[...] = jnp.zeros((1, KP), F32)
    ep[:, :ROWS] = e_ref[...]

    vb_load.wait()
    own = pl.ds(mult(n, BW), BW)
    for i in range(KP // 128):
        vbt[own, i * 128 : (i + 1) * 128] = vb[i * 128 : (i + 1) * 128, :].T[:BW, :]
    pl.semaphore_wait(barrier, 15)

    def ag(src_n, half, to, slot):
        rows = pl.ds(mult(src_n * 2 + half, 32), 32)
        return remote(vbt.at[rows], vbt.at[rows], ag_s.at[slot], ag_r.at[src_n * 2 + half], narrow_peer(to))

    zp = zbase + y
    sends = [
        (n, 0, zp, 0), (n, 0, yp, 2), (n, 1, ym, 3), (n, 1, zp, 1), (n, 1, yp, 4), (n, 0, ym, 5),
    ]
    forwards = [(ym, 0, yp, 6), (yp, 1, ym, 7)]
    zsends = [(zp, 0, yp, 8), (zp, 1, ym, 9), (zp, 1, yp, 10), (zp, 0, ym, 11)]
    zym, zyp = zbase + lax.rem(y + 3, 4), zbase + lax.rem(y + 1, 4)
    zforwards = [(zym, 0, yp, 12), (zyp, 1, ym, 13)]

    def ag_arrived(src_n, half):
        ag(src_n, half, yp, 0).wait_recv()

    for m in sends:
        ag(*m).start()

    r_load.wait()

    @pl.loop(0, KP // 128)
    def _(i):
        rows = pl.ds(mult(i, 128), 128)
        for j in range(2):
            hi, lo = split(r[rows, j * 128 : (j + 1) * 128].T)
            rtr[0, j * 128 : (j + 1) * 128, rows] = hi
            rtr[1, j * 128 : (j + 1) * 128, rows] = lo

    myrows = pl.ds(mult(c, 128), 128)
    hisrows = pl.ds(mult(1 - c, 128), 128)

    def x_copy(st, i):
        cols = pl.ds(mult(i, 256), 256)
        return remote(
            part.at[st, hisrows, cols], xrecv.at[st, :, cols], xs.at[st * 4 + i], xr.at[st * 4 + i], partner
        )

    def rs_copy(st, kk):
        return remote(
            part.at[st, myrows, pl.ds(mult(kk, 128), 128)], rsr.at[st, k], rs_s.at[st * 8 + kk],
            rs_r.at[st * 8 + k], same_core(kk),
        )

    def reduce_start(st, compute):
        def finish(i):
            cols = pl.ds(mult(i, 256), 256)
            x_copy(st, i).wait_recv()
            part[st, myrows, cols] = part[st, myrows, cols] + xrecv[st, :, cols]
            for t in range(2):
                kk = 2 * i + t

                @pl.when(kk != k)
                def _():
                    rs_copy(st, kk).start()

        @pl.loop(0, 4)
        def _(s):
            i = order(s)
            part[st, :, pl.ds(mult(i, 256), 256)] = compute(i)
            x_copy(st, i).start()

            @pl.when(s >= 1)
            def _():
                finish(order(s - 1))

        finish(order(3))

    def reduce_end(st):
        total = part[st, myrows, pl.ds(mult(k, 128), 128)]
        for d in range(1, 8):
            kk = lax.rem(k + d, 8)
            remote(rsr.at[st, kk], rsr.at[st, kk], rs_s.at[st * 8], rs_r.at[st * 8 + kk], partner).wait_recv()
            total = total + rsr[st, kk]
        return total

    def reduce_drain(st):
        for i in range(4):
            x_copy(st, i).wait_send()
        for d in range(1, 8):
            rs_copy(st, lax.rem(k + d, 8)).wait_send()

    def project(i):
        v_load(i).wait()
        return dot3((rtr[0], rtr[1]), split(v[:, pl.ds(mult(i, 256), 256)]))

    reduce_start(0, project)

    tt = split(t_ref[...])
    ttt = split(t_ref[...].T)

    @pl.loop(0, 4)
    def _(i):
        rows = pl.ds(mult(i, 512), 512)
        hi, lo = split(dot3(split(r[rows, :]), tt))
        rt[0, rows, :] = hi
        rt[1, rows, :] = lo
        hi, lo = split(dot3(ttt, (rtr[0, :, rows], rtr[1, :, rows])))
        rtt[0, :, rows] = hi
        rtt[1, :, rows] = lo

    for m in forwards:
        ag_arrived(m[0], m[1])
        ag(*m).start()

    def pa_copy(kk):
        cols = pl.ds(mult(k, 128), 128)
        return remote(pred, pfull.at[myrows, cols], pa_s.at[kk], pa_r.at[k], same_core(kk))

    def relay(kk):
        cols = pl.ds(mult(kk, 128), 128)
        return remote(
            pfull.at[myrows, cols], pfull.at[myrows, cols], pr_s.at[kk], pr_r.at[kk], partner
        )

    total = reduce_end(0)
    pred[...] = total
    pfull[myrows, pl.ds(mult(k, 128), 128)] = total
    for d in range(1, 8):
        pa_copy(lax.rem(k + d, 8)).start()
    relay(k).start()

    ag_arrived(zp, 0)
    ag_arrived(zp, 1)
    for m in zsends:
        ag(*m).start()

    for d in range(1, 8):
        kk = lax.rem(k + d, 8)
        remote(pred, pred, pa_s.at[0], pa_r.at[kk], partner).wait_recv()
        relay(kk).start()
    for kk in range(8):
        remote(pred, pred, pr_s.at[0], pr_r.at[kk], partner).wait_recv()

    for j in range(2):
        pbt[own, j * 128 : (j + 1) * 128] = pfull[j * 128 : (j + 1) * 128, OFF : OFF + 128].T[:BW, :]

    def pb_copy(nn):
        return remote(pbt.at[own], pbt.at[own], pb_s.at[nn], pb_r.at[n], narrow_peer(nn))

    for d in range(1, 8):
        pb_copy(lax.rem(n + d, 8)).start()

    def u_store(j):
        cols = pl.ds(mult(j, 256), 256)
        return pltpu.make_async_copy(v.at[pl.ds(0, ROWS), cols], u_hbm.at[:, cols], out_sem.at[j])

    @pl.loop(0, 4)
    def _(j):
        cols = pl.ds(mult(j, 256), 256)
        pj = split(pfull[:, cols])

        @pl.loop(0, 4)
        def _(i):
            rows = pl.ds(mult(i, 512), 512)
            u = v[rows, cols] - dot3((rt[0, rows, :], rt[1, rows, :]), pj)
            v[rows, cols] = u
            hi, lo = split(u)
            uu[0, rows, cols] = hi
            uu[1, rows, cols] = lo

        u_store(j).start()

    for m in zforwards:
        ag_arrived(m[0], m[1])
        ag(*m).start()
    for d in range(1, 8):
        nn = lax.rem(n + d, 8)
        remote(pbt.at[own], pbt.at[own], pb_s.at[0], pb_r.at[nn], partner).wait_recv()

    def f_copy(h, col):
        return remote(
            fsend.at[h], fo.at[:, pl.ds(pl.multiple_of(col, 128), 128)], f_s.at[h], f_r.at[h], partner
        )

    def fock(h, hb):
        @pl.loop(0, 4)
        def _(i):
            cols = pl.ds(mult(i, 512), 512)
            rows = pl.ds(mult(hb, 256), 256)
            p = split(pbt[rows, :])
            x = (vbt[rows, cols] - dot3(p, (rtt[0, :, cols], rtt[1, :, cols]))) * ep[:, cols]
            hi, lo = split(x)
            ub[0, :, cols] = hi
            ub[1, :, cols] = lo

        def compute(i):
            cols = pl.ds(mult(i, 256), 256)
            return dot3((ub[0], ub[1]), (uu[0, :, cols], uu[1, :, cols]))

        reduce_start(1 + h, compute)

    def fock_end(h, hb):
        red[...] = reduce_end(1 + h).T
        col = hb * 256 + c * 128
        fo[:, pl.ds(pl.multiple_of(col, 128), 128)] = red[pl.ds(mult(c, BW), BW), :]
        fsend[h] = red[pl.ds(mult(1 - c, BW), BW), :]
        f_copy(h, col).start()

    for d in (1, 2, 3):
        src = base + lax.rem(y + d, 4)
        for half in range(2):
            if (d == 3 and half == 0) or (d == 1 and half == 1):
                continue
            ag_arrived(src, half)
    fock(0, zh)
    for d in (1, 2, 3):
        src = zbase + lax.rem(y + d, 4)
        for half in range(2):
            if (d == 3 and half == 0) or (d == 1 and half == 1):
                continue
            ag_arrived(src, half)
    fock_end(0, zh)
    fock(1, 1 - zh)
    fock_end(1, 1 - zh)
    for h in range(2):
        f_copy(h, 0).wait_recv()
    f_ref[...] = fo[...]

    for h in range(2):
        f_copy(h, 0).wait_send()
    for m in sends + forwards + zsends + zforwards:
        ag(*m).wait_send()
    for st in range(3):
        reduce_drain(st)
    for d in range(1, 8):
        pa_copy(lax.rem(k + d, 8)).wait_send()
        pb_copy(lax.rem(n + d, 8)).wait_send()
    for kk in range(8):
        relay(kk).wait_send()
    for j in range(4):
        u_store(j).wait()


def on_device(vectors, reflectors, triangle, energies):
    vm = pl.BlockSpec(memory_space=pltpu.VMEM)
    hbm = pl.BlockSpec(memory_space=pl.ANY)
    dma = pltpu.SemaphoreType.DMA
    return pl.pallas_call(
        kernel,
        out_shape=(
            jax.ShapeDtypeStruct((ROWS, NC), F32),
            jax.ShapeDtypeStruct((BW, FB), F32),
        ),
        in_specs=[hbm, hbm, vm, vm],
        out_specs=(hbm, vm),
        scratch_shapes=[
            pltpu.VMEM((KP, NC), F32),
            pltpu.VMEM((KP, NB), F32),
            pltpu.VMEM((KP, 128), F32),
            pltpu.VMEM((2, NB, KP), BF16),
            pltpu.VMEM((2, KP, NB), BF16),
            pltpu.VMEM((2, NB, KP), BF16),
            pltpu.VMEM((2, KP, NC), BF16),
            pltpu.VMEM((FB, KP), F32),
            pltpu.VMEM((FB, NB), F32),
            pltpu.VMEM((1, KP), F32),
            pltpu.VMEM((3, 256, NC), F32),
            pltpu.VMEM((3, 128, NC), F32),
            pltpu.VMEM((3, 8, 128, 128), F32),
            pltpu.VMEM((128, 128), F32),
            pltpu.VMEM((NB, NC), F32),
            pltpu.VMEM((2, 256, KP), BF16),
            pltpu.VMEM((128, 128), F32),
            pltpu.VMEM((BW, FB), F32),
            pltpu.VMEM((2, BW, 128), F32),
            dma((6,)), dma((4,)), dma((14,)), dma((16,)), dma((12,)), dma((12,)),
            dma((24,)), dma((24,)), dma((8,)), dma((8,)), dma((8,)), dma((8,)),
            dma((8,)), dma((8,)), dma((2,)), dma((2,)),
        ],
        compiler_params=pltpu.CompilerParams(
            collective_id=0, has_side_effects=True, vmem_limit_bytes=56 * 2**20
        ),
        name="reflect_fock",
    )(vectors, reflectors, triangle, energies[None, :])


def solution(mesh):
    return jax.shard_map(
        on_device,
        mesh=mesh,
        in_specs=(P("wide", "narrow"), P("wide", None), P(), P("wide")),
        out_specs=(P("wide", "narrow"), P(("narrow", "wide"), None)),
        check_vma=False,
    )
```

time: 332 us -> 85 us (0.26)
  waiting for transfers between devices: 255 us -> 0 us
  Pallas kernels: 0 us -> 75.3 us
  matrix products: 53.8 us -> 0 us
  between operations: 13.8 us -> 0.65 us
    psum x1 -> x0, waiting for transfers between devices: 123 us -> none  [on_device(): projected = lax.psum(partial_proj, 'wide')]
    pallas_call x0 -> x1, Pallas kernels: none -> 75.3 us  [on_device(): pl.pallas_call(kernel, out_shape=(jax.ShapeDtypeStruct((ROWS, NC), F32),...]
    all_gather x1 -> x0, waiting for transfers between devices: 72.3 us -> none  [on_device(): lax.all_gather(own_columns, 'narrow', axis=1, tiled=True)]
    reduce_scatter x1 -> x0, waiting for transfers between devices: 59 us -> none  [on_device(): lax.psum_scatter(fock_part, 'wide', scatter_dimension=0, tiled=True)]
    dot_general x4 -> x0, matrix products: 53.8 us -> none  [the longest x1 30.9 us: on_device(): lax.dot_general(updated, scaled_rows * lax.all_gather(own_columns, 'narro...]
    unnamed x8 -> x4, local copies, waits for them, and re-layouts: 4.85 us -> 8.96 us
  transfers between devices with their start and end apart: 3 -> 0, of which waited for: 3 -> 0; matrix products, arithmetic and copies ran while one was open for 0% -> 0% of each run, Pallas kernels for 0% -> 0%
where the time goes in v1:
time: 85 us; the launch traced here: 84.9 us
  Pallas kernels  75.3 us (89%)
  local copies, waits for them, and re-layouts  8.96 us (11%)
    pallas_call x1, Pallas kernels, on_device(): pl.pallas_call(kernel, out_shape=(jax.ShapeDtypeStruct((ROWS, NC), F32),...  75.3 us
    unnamed x4, local copies, waits for them, and re-layouts  8.96 us

profile of v1, /device:TPU:1, one launch (start us, length us, event | category | flops | bytes accessed | tf_op | source)
XLA Modules:
  0.0 84.9 jit_solution(15472629311695092087)
XLA Ops:
  0.6 75.3 %reflect_fock.1 = (f32[2000,1024]{1,0:T(8,128)}, f32[64,512]{1,0:T(8,128)}) custom-call(f32[2000,1024]{1,0:T(8,128)} %v_hbm.1, f32[2000,256]{1,0:T(8,128)} %r_hbm.1, f32[256,256]{1,0:T(8,128)} %t_ref.1, f32[1,2000]{1,0:T(1,128)} %bitcast.1), custom_call_target="tpu_custom_call" | custom-call | tf_op jit(solution)/shard_map/reflect_fock/pallas_call | solution.py:330
  76.0 0.0 copy-start
  76.0 8.3 %copy.8 = f32[2000,1024]{1,0:T(8,128)} copy(f32[2000,1024]{1,0:T(8,128)} %get-tuple-element.4) | data formatting | bytes 16384000
  84.3 0.0 copy-done
  84.3 0.7 copy.9
Async XLA Ops:
  76.0 8.3 %copy-start = (f32[64,512]{1,0:T(8,128)S(1)}, f32[64,512]{1,0:T(8,128)}, u32[]{:S(2)}) copy-start(f32[64,512]{1,0:T(8,128)} %get-tuple-element.5) | copy-start | bytes 393220

commit v2 on v1

v2 whole, which is shorter than its diff:
```python
import functools

import jax
import jax.numpy as jnp
from jax import lax
from jax.experimental import pallas as pl
from jax.experimental.pallas import tpu as pltpu
from jax.sharding import PartitionSpec as P

MESH = pl.DeviceIdType.MESH
F32, BF16 = jnp.float32, jnp.bfloat16
ROWS, KP, NC, NB = 2000, 2048, 1024, 256
FB, OFF, BW = 512, 256, 64
M0, M1 = 320, 192


def dot(a, b):
    return jnp.dot(a, b, preferred_element_type=F32)


def split(x):
    hi = x.astype(BF16)
    return hi, (x - hi.astype(F32)).astype(BF16)


def dot3(a, b):
    return dot(a[0], b[0]) + dot(a[0], b[1]) + dot(a[1], b[0])


def mult(i, m):
    return pl.multiple_of(i * m, m)


def kernel(
    v_hbm, r_hbm, t_hbm, e_hbm, u_out, f_out,
    v, r, vb, t_ref, e_ref, rtr, rt, rtt, uu, vbt, pbt, ep, part0, part1, part2, xrecv0, xrecv1, xrecv2,
    rsr0, rsr1, rsr2, pfull, ub, fl, fg, ft,
    ld_sem, ag_s, ag_r, xs, xr, rs_s, rs_r, pa_s, pa_r, pr_s, pr_r, pb_s, pb_r, f_s, f_r,
):
    w, n = lax.axis_index("wide"), lax.axis_index("narrow")
    c, k = lax.rem(w, 2), w // 2
    y, zh = lax.rem(n, 4), n // 4
    partner = (w + 1 - 2 * c, n)
    yp, ym = zh * 4 + lax.rem(y + 1, 4), zh * 4 + lax.rem(y + 3, 4)
    base = zh * 4
    zbase = (1 - zh) * 4

    def same_core(kk):
        return (2 * kk + c, n)

    def narrow_peer(nn):
        return (w, nn)

    def remote(src, dst, s, rsem, to):
        return pltpu.make_async_remote_copy(
            src_ref=src, dst_ref=dst, send_sem=s, recv_sem=rsem, device_id=to, device_id_type=MESH
        )

    kk0 = k // 2

    def order(s):
        return lax.rem(kk0 + 1 + s, 4)

    vb_load = pltpu.make_async_copy(v_hbm.at[:, pl.ds(OFF, 128)], vb.at[pl.ds(0, ROWS)], ld_sem.at[0])
    r_load = pltpu.make_async_copy(r_hbm, r.at[pl.ds(0, ROWS)], ld_sem.at[1])

    def v_load(i):
        cols = pl.ds(mult(i, 256), 256)
        return pltpu.make_async_copy(v_hbm.at[:, cols], v.at[pl.ds(0, ROWS), cols], ld_sem.at[2 + i])

    t_load = pltpu.make_async_copy(t_hbm, t_ref, ld_sem.at[6])
    e_load = pltpu.make_async_copy(e_hbm, e_ref, ld_sem.at[7])
    vb_load.start()
    r_load.start()
    for s in range(4):
        v_load(order(s)).start()
    t_load.start()
    e_load.start()

    barrier = pltpu.get_barrier_semaphore()
    pl.semaphore_signal(barrier, inc=1, device_id=partner, device_id_type=MESH)
    for d in range(1, 8):
        pl.semaphore_signal(barrier, inc=1, device_id=same_core(lax.rem(k + d, 8)), device_id_type=MESH)
        pl.semaphore_signal(barrier, inc=1, device_id=narrow_peer(lax.rem(n + d, 8)), device_id_type=MESH)

    vb[ROWS:, :] = jnp.zeros((KP - ROWS, 128), F32)
    r[ROWS:, :] = jnp.zeros((KP - ROWS, NB), F32)
    v[ROWS:, :] = jnp.zeros((KP - ROWS, NC), F32)

    vb_load.wait()
    own = pl.ds(mult(n, BW), BW)
    for i in range(KP // 128):
        vbt[own, i * 128 : (i + 1) * 128] = vb[i * 128 : (i + 1) * 128, :].T[:BW, :]
    pl.semaphore_wait(barrier, 15)

    def ag(src_n, o, cnt, to, slot):
        rows = pl.ds(mult(src_n * 8 + o, 8), 8 * cnt)
        return remote(vbt.at[rows], vbt.at[rows], ag_s.at[slot], ag_r.at[src_n * 8 + o], narrow_peer(to))

    def arrived(src_n, o, cnt):
        ag(src_n, o, cnt, yp, 0).wait_recv()

    zp = zbase + y
    zyp, zym = zbase + lax.rem(y + 1, 4), zbase + lax.rem(y + 3, 4)
    y2, zy2 = base + lax.rem(y + 2, 4), zbase + lax.rem(y + 2, 4)
    z_sends = [(n, 2 * q, 2, zp, q) for q in range(4)]
    zx_sends = [(ym, 6, 2, zp, 4), (yp, 6, 2, zp, 5), (y2, 6, 2, zp, 6)]
    y_sends = [(n, 0, 4, yp, 7), (n, 0, 4, ym, 8), (n, 4, 4, yp, 9), (n, 4, 4, ym, 10)]
    y_fwds = [(ym, 0, 2, yp, 11), (yp, 2, 2, ym, 12), (ym, 4, 2, yp, 13), (yp, 6, 2, ym, 14)]
    p_sends = [(zp, 0, 4, yp, 15), (zp, 0, 4, ym, 16), (zp, 4, 2, yp, 17), (zp, 4, 2, ym, 18)]
    p_fwds = [(zym, 0, 2, yp, 19), (zyp, 2, 2, ym, 20), (zym, 4, 1, yp, 21), (zyp, 5, 1, ym, 22)]
    every = z_sends + zx_sends + y_sends + y_fwds + p_sends + p_fwds

    def go(messages):
        for m in messages:
            ag(*m).start()

    go(z_sends[:1] + y_sends)

    r_load.wait()

    @pl.loop(0, 4)
    def _(i):
        rows = pl.ds(mult(i, 512), 512)
        hi, lo = split(r[rows, :])
        rtr[0, :, rows] = hi.T
        rtr[1, :, rows] = lo.T

    part, xrecv, rsr = (part0, part1, part2), (xrecv0, xrecv1, xrecv2), (rsr0, rsr1, rsr2)
    half_rows = (128, M0 // 2, M1 // 2)
    myrows = pl.ds(mult(c, 128), 128)
    hisrows = pl.ds(mult(1 - c, 128), 128)

    def mine(st):
        return pl.ds(mult(c, half_rows[st]), half_rows[st])

    def his(st):
        return pl.ds(mult(1 - c, half_rows[st]), half_rows[st])

    def x_copy(st, i):
        cols = pl.ds(mult(i, 256), 256)
        return remote(
            part[st].at[his(st), cols], xrecv[st].at[:, cols], xs.at[st * 4 + i], xr.at[st * 4 + i], partner
        )

    def rs_copy(st, kk):
        return remote(
            part[st].at[mine(st), pl.ds(mult(kk, 128), 128)], rsr[st].at[k], rs_s.at[st * 8 + kk],
            rs_r.at[st * 8 + k], same_core(kk),
        )

    def finish(st, i):
        cols = pl.ds(mult(i, 256), 256)
        x_copy(st, i).wait_recv()
        part[st][mine(st), cols] = part[st][mine(st), cols] + xrecv[st][:, cols]
        for t in range(2):
            kk = 2 * i + t

            @pl.when(kk != k)
            def _():
                rs_copy(st, kk).start()

    def reduce_start(st, compute, hooks=()):
        @pl.loop(0, 4)
        def _(s):
            i = order(s)
            part[st][:, pl.ds(mult(i, 256), 256)] = compute(i)
            x_copy(st, i).start()

            @pl.when(s >= 1)
            def _():
                finish(st, order(s - 1))

            for at, hook in hooks:

                @pl.when(s == at)
                def _():
                    hook()

    def reduce_end(st):
        total = part[st][mine(st), pl.ds(mult(k, 128), 128)]
        for d in range(1, 8):
            kk = lax.rem(k + d, 8)
            remote(rsr[st].at[kk], rsr[st].at[kk], rs_s.at[st * 8], rs_r.at[st * 8 + kk], partner).wait_recv()
            total = total + rsr[st][kk]
        return total

    def reduce_drain(st):
        for i in range(4):
            x_copy(st, i).wait_send()
        for d in range(1, 8):
            rs_copy(st, lax.rem(k + d, 8)).wait_send()

    def project(i):
        v_load(i).wait()
        return dot3((rtr[0], rtr[1]), split(v[:, pl.ds(mult(i, 256), 256)]))

    reduce_start(0, project)

    t_load.wait()
    e_load.wait()
    ep[...] = jnp.zeros((1, KP), F32)
    ep[:, :ROWS] = e_ref[...]
    tt = split(t_ref[...])
    ttt = split(t_ref[...].T)

    @pl.loop(0, 2)
    def _(i):
        rows = pl.ds(mult(i, 1024), 1024)
        hi, lo = split(dot3(split(r[rows, :]), tt))
        rt[0, rows, :] = hi
        rt[1, rows, :] = lo

        @pl.when(i == 0)
        def _():
            finish(0, order(3))
            go(z_sends[1:2])

    @pl.loop(0, 2)
    def _(i):
        rows = pl.ds(mult(i, 1024), 1024)
        hi, lo = split(dot3(ttt, (rtr[0, :, rows], rtr[1, :, rows])))
        rtt[0:256, rows] = hi
        rtt[256:512, rows] = lo
        rtt[512:768, rows] = hi

    arrived(ym, 0, 4)
    arrived(yp, 0, 4)
    go(y_fwds[:2])

    x, zl = lax.rem(k, 4), k // 4
    kz = (1 - zl) * 4 + x

    def slice_copy(src_k, to_k, slot):
        cols = pl.ds(mult(src_k, 128), 128)
        return remote(
            pfull.at[myrows, cols], pfull.at[myrows, cols], pa_s.at[slot], pa_r.at[src_k], same_core(to_k)
        )

    x_peers = [zl * 4 + lax.rem(x + d, 4) for d in (1, 3, 2)]
    slices = [(k, kz, 0)] + [(k, kx, 1 + d) for d, kx in enumerate(x_peers)]
    z_slices = [(kz, kx, 4 + d) for d, kx in enumerate(x_peers)]

    def slice_here(kk):
        slice_copy(kk, kz, 0).wait_recv()

    def relay(kk):
        cols = pl.ds(mult(kk, 128), 128)
        return remote(
            pfull.at[myrows, cols], pfull.at[myrows, cols], pr_s.at[kk], pr_r.at[kk], partner
        )

    total = reduce_end(0)
    pfull[myrows, pl.ds(mult(k, 128), 128)] = total
    for m in slices:
        slice_copy(*m).start()
    relay(k).start()
    go(z_sends[2:])
    arrived(ym, 4, 4)
    arrived(yp, 4, 4)
    go(y_fwds[2:])
    slice_here(kz)
    for m in z_slices:
        slice_copy(*m).start()
    relay(kz).start()
    arrived(zp, 0, 2)
    arrived(zp, 2, 2)
    go(p_sends[:2])
    for kx in x_peers:
        slice_here(kx)
        relay(kx).start()
    def relay_in(kk):
        cols = pl.ds(mult(kk, 128), 128)
        return remote(pfull.at[hisrows, cols], pfull.at[hisrows, cols], pr_s.at[0], pr_r.at[kk], partner)

    def slice_arrived(kk):
        relay_in(kk).wait_recv()

    def pb_rows(nn, cc):
        return pbt.at[pl.ds(mult(2 * nn + cc, 32), 32)]

    def pb_copy(nn):
        return remote(pb_rows(n, c), pb_rows(n, c), pb_s.at[nn], pb_r.at[n], narrow_peer(nn))

    def pb_in(nn):
        return remote(pb_rows(nn, c), pb_rows(nn, c), pb_s.at[0], pb_r.at[nn], partner)

    def pb_relay(nn, cc):
        return remote(pb_rows(nn, cc), pb_rows(nn, cc), pb_s.at[8 + nn], pb_r.at[8 + nn], partner)

    peers = [base + lax.rem(y + d, 4) for d in (1, 3, 2)] + [zp, zyp, zym, zy2]

    def pb_send():
        for j in range(2):
            pbt[own, j * 128 : (j + 1) * 128] = pfull[j * 128 : (j + 1) * 128, OFF : OFF + 128].T[:BW, :]
        for nn in peers:
            pb_copy(nn).start()

    uu[0, ROWS:, :] = jnp.zeros((KP - ROWS, NC), BF16)
    uu[1, ROWS:, :] = jnp.zeros((KP - ROWS, NC), BF16)

    def update(zz):
        @pl.loop(0, 2)
        def _(j):
            cols = pl.ds(mult(2 * zz + j, 256), 256)
            p = split(pfull[:, cols])
            u = v[:ROWS, cols] - dot3((rt[0, :ROWS, :], rt[1, :ROWS, :]), p)
            u_out[:, cols] = u
            hi, lo = split(u)
            uu[0, :ROWS, cols] = hi
            uu[1, :ROWS, cols] = lo

    for kx in [k] + x_peers:
        slice_arrived(kx)

    @pl.when(zl == 0)
    def _():
        pb_send()

    update(zl)
    z_peers = [(1 - zl) * 4 + lax.rem(x + d, 4) for d in (1, 3, 2)]
    for kx in z_peers:
        slice_here(kx)
        relay(kx).start()
    for kx in [kz] + z_peers:
        slice_arrived(kx)

    @pl.when(zl == 1)
    def _():
        pb_send()

    arrived(zp, 4, 2)
    go(p_sends[2:])
    arrived(y2, 6, 2)
    go(zx_sends)
    update(1 - zl)
    arrived(zym, 0, 4)
    arrived(zyp, 0, 4)
    go(p_fwds[:2])
    for nn in peers:
        pb_in(nn).wait_recv()
        pb_relay(nn, c).start()
    for nn in peers:
        pb_relay(nn, 1 - c).wait_recv()

    blocks = [base + d for d in range(4)] + [zp, zyp, zy2, zym]

    def f_copy(h):
        first = h * M0
        rows = pl.ds(pl.multiple_of(first + c * half_rows[1 + h], 32), half_rows[1 + h])
        return remote(fl.at[rows], fl.at[rows], f_s.at[h], f_r.at[h], partner)

    def fock(h, hooks=()):
        srcs = [pl.ds(mult(nn, BW), BW) for nn in (blocks[:5] if h == 0 else blocks[5:])]
        if h == 0:
            srcs = [pl.ds(mult(zh, 4 * BW), 4 * BW)] + srcs[4:]
        hi, lo = split(jnp.concatenate([pbt[src, :] for src in srcs], axis=0))
        p = jnp.concatenate([hi, hi, lo], axis=1)

        @pl.loop(0, 2)
        def _(i):
            cols = pl.ds(mult(i, 1024), 1024)
            vv = jnp.concatenate([vbt[src, cols] for src in srcs], axis=0)
            hi, lo = split((vv - dot(p, rtt[:, cols])) * ep[:, cols])
            ub[0, : hi.shape[0], cols] = hi
            ub[1, : hi.shape[0], cols] = lo

        m = M0 if h == 0 else M1

        def compute(i):
            cols = pl.ds(mult(i, 256), 256)
            return dot3((ub[0, :m], ub[1, :m]), (uu[0, :, cols], uu[1, :, cols]))

        reduce_start(1 + h, compute, hooks)

    def fock_end(h):
        first = h * M0
        rows = pl.ds(pl.multiple_of(first + c * half_rows[1 + h], 32), half_rows[1 + h])
        fl[rows, :] = reduce_end(1 + h)
        f_copy(h).start()

    for o in (0, 2, 4):
        arrived(y2, o, 2)
    arrived(zp, 6, 2)

    def pass_last():
        arrived(zym, 4, 2)
        arrived(zyp, 4, 2)
        go(p_fwds[2:])

    fock(0, [(0, pass_last)])
    arrived(zym, 6, 2)
    arrived(zyp, 6, 2)
    for o, cnt in ((0, 2), (2, 2), (4, 1), (5, 1), (6, 2)):
        arrived(zy2, o, cnt)
    fock(1, [(0, lambda: finish(1, order(3)))])
    finish(2, order(3))
    fock_end(0)
    fock_end(1)
    def f_in(h):
        rows = pl.ds(pl.multiple_of(h * M0 + (1 - c) * half_rows[1 + h], 32), half_rows[1 + h])
        return remote(fl.at[rows], fl.at[rows], f_s.at[h], f_r.at[h], partner)

    for h in range(2):
        f_in(h).wait_recv()
    for at, nn in enumerate(blocks):
        fg[pl.ds(mult(nn, BW), BW), :] = fl[at * BW : (at + 1) * BW, :]
    ft[...] = fg[...].T
    f_out[...] = ft[pl.ds(mult(c, BW), BW), :]

    for h in range(2):
        f_copy(h).wait_send()
    for m in every:
        ag(*m).wait_send()
    for st in range(3):
        reduce_drain(st)
    for m in slices + z_slices:
        slice_copy(*m).wait_send()
    for nn in peers:
        pb_copy(nn).wait_send()
        pb_relay(nn, c).wait_send()
    for kk in range(8):
        relay(kk).wait_send()


def on_device(vectors, reflectors, triangle, energies):
    vm = pl.BlockSpec(memory_space=pltpu.VMEM)
    hbm = pl.BlockSpec(memory_space=pl.ANY)
    dma = pltpu.SemaphoreType.DMA
    return pl.pallas_call(
        kernel,
        out_shape=(
            pltpu.VMEM((ROWS, NC), F32),
            pltpu.VMEM((BW, FB), F32),
        ),
        in_specs=[hbm, hbm, hbm, hbm],
        out_specs=(vm, vm),
        scratch_shapes=[
            pltpu.VMEM((KP, NC), F32),
            pltpu.VMEM((KP, NB), F32),
            pltpu.VMEM((KP, 128), F32),
            pltpu.VMEM((NB, NB), F32),
            pltpu.VMEM((1, ROWS), F32),
            pltpu.VMEM((2, NB, KP), BF16),
            pltpu.VMEM((2, KP, NB), BF16),
            pltpu.VMEM((3 * NB, KP), BF16),
            pltpu.VMEM((2, KP, NC), BF16),
            pltpu.VMEM((FB, KP), F32),
            pltpu.VMEM((FB, NB), F32),
            pltpu.VMEM((1, KP), F32),
            pltpu.VMEM((NB, NC), F32),
            pltpu.VMEM((M0, NC), F32),
            pltpu.VMEM((M1, NC), F32),
            pltpu.VMEM((128, NC), F32),
            pltpu.VMEM((M0 // 2, NC), F32),
            pltpu.VMEM((M1 // 2, NC), F32),
            pltpu.VMEM((8, 128, 128), F32),
            pltpu.VMEM((8, M0 // 2, 128), F32),
            pltpu.VMEM((8, M1 // 2, 128), F32),
            pltpu.VMEM((NB, NC), F32),
            pltpu.VMEM((2, M0, KP), BF16),
            pltpu.VMEM((FB, 128), F32),
            pltpu.VMEM((FB, 128), F32),
            pltpu.VMEM((128, FB), F32),
            dma((8,)), dma((23,)), dma((64,)), dma((12,)), dma((12,)),
            dma((24,)), dma((24,)), dma((8,)), dma((8,)), dma((8,)), dma((8,)),
            dma((16,)), dma((16,)), dma((2,)), dma((2,)),
        ],
        compiler_params=pltpu.CompilerParams(
            collective_id=0, has_side_effects=True, vmem_limit_bytes=50 * 2**20
        ),
        name="reflect_fock",
    )(vectors, reflectors, triangle, energies[None, :])


def solution(mesh):
    return jax.shard_map(
        on_device,
        mesh=mesh,
        in_specs=(P("wide", "narrow"), P("wide", None), P(), P("wide")),
        out_specs=(P("wide", "narrow"), P(("narrow", "wide"), None)),
        check_vma=False,
    )
```

time: 85 us -> 65.6 us (0.77)
  Pallas kernels: 75.3 us -> 60.8 us
  local copies, waits for them, and re-layouts: 8.96 us -> 3.99 us
    pallas_call x1, Pallas kernels: 75.3 us -> 60.8 us  [on_device(): pl.pallas_call(kernel, out_shape=(pltpu.VMEM((ROWS, NC), F32), pltpu.VMEM...]
    unnamed x4 -> x2, local copies, waits for them, and re-layouts: 8.96 us -> 3.99 us
where the time goes in v2:
time: 65.6 us; the launch traced here: 65.5 us
  Pallas kernels  60.8 us (93%)
  local copies, waits for them, and re-layouts  3.99 us (6%)
    pallas_call x1, Pallas kernels, on_device(): pl.pallas_call(kernel, out_shape=(pltpu.VMEM((ROWS, NC), F32), pltpu.VMEM...  60.8 us
    unnamed x2, local copies, waits for them, and re-layouts  3.99 us

profile of v2, /device:TPU:1, one launch (start us, length us, event | category | flops | bytes accessed | tf_op | source)
XLA Modules:
  0.0 65.5 jit_solution(10005985813656155007)
XLA Ops:
  0.6 60.8 %reflect_fock.1 = (f32[2000,1024]{1,0:T(8,128)S(1)}, f32[64,512]{1,0:T(8,128)S(1)}) custom-call(f32[2000,1024]{1,0:T(8,128)} %v_hbm.1, f32[2000,256]{1,0:T(8,128)} %r_hbm.1, f32[256,256]{1,0:T(8,128)} %t_hbm.1, f32[1,2000]{1,0:T(1,128)} %bitcast.1), custom_call_target="tpu_custom_call" | custom-call | tf_op jit(solution)/shard_map/reflect_fock/pallas_call | solution.py:430
  61.5 3.3 %copy.8 = f32[2000,1024]{1,0:T(8,128)} copy(f32[2000,1024]{1,0:T(8,128)S(1)} %get-tuple-element.2) | data formatting | bytes 16384000
  64.8 0.7 %copy.9 = f32[64,512]{1,0:T(8,128)} copy(f32[64,512]{1,0:T(8,128)S(1)} %get-tuple-element.3) | data formatting | bytes 262144

commit v3 on v2

--- a/solution.py
+++ b/solution.py
@@ -11,7 +11,8 @@
 F32, BF16 = jnp.float32, jnp.bfloat16
 ROWS, KP, NC, NB = 2000, 2048, 1024, 256
 FB, OFF, BW = 512, 256, 64
-M0, M1 = 320, 192
+PARTS = (256, 192, 64)
+KB = OFF // 128
 
 
 def dot(a, b):
@@ -33,8 +34,8 @@
 
 def kernel(
     v_hbm, r_hbm, t_hbm, e_hbm, u_out, f_out,
-    v, r, vb, t_ref, e_ref, rtr, rt, rtt, uu, vbt, pbt, ep, part0, part1, part2, xrecv0, xrecv1, xrecv2,
-    rsr0, rsr1, rsr2, pfull, ub, fl, fg, ft,
+    v, r, vb, t_ref, e_ref, rtr, rt, yt, a3, a4, bb, uu, vbt, pbt, ep, part0, part1, part2, part3, xrecv0, xrecv1, xrecv2,
+    xrecv3, rsr0, rsr1, rsr2, rsr3, pfull, ub, fl, fg, ft,
     ld_sem, ag_s, ag_r, xs, xr, rs_s, rs_r, pa_s, pa_r, pr_s, pr_r, pb_s, pb_r, f_s, f_r,
 ):
     w, n = lax.axis_index("wide"), lax.axis_index("narrow")
@@ -59,7 +60,9 @@
     kk0 = k // 2
 
     def order(s):
-        return lax.rem(kk0 + 1 + s, 4)
+        t1, t0 = (3 - s) // 2, lax.rem(3 - s, 2)
+        a, b = kk0 // 2, lax.rem(kk0, 2)
+        return 2 * (a + t1 - 2 * a * t1) + b + t0 - 2 * b * t0
 
     vb_load = pltpu.make_async_copy(v_hbm.at[:, pl.ds(OFF, 128)], vb.at[pl.ds(0, ROWS)], ld_sem.at[0])
     r_load = pltpu.make_async_copy(r_hbm, r.at[pl.ds(0, ROWS)], ld_sem.at[1])
@@ -104,11 +107,14 @@
     zyp, zym = zbase + lax.rem(y + 1, 4), zbase + lax.rem(y + 3, 4)
     y2, zy2 = base + lax.rem(y + 2, 4), zbase + lax.rem(y + 2, 4)
     z_sends = [(n, 2 * q, 2, zp, q) for q in range(4)]
-    zx_sends = [(ym, 6, 2, zp, 4), (yp, 6, 2, zp, 5), (y2, 6, 2, zp, 6)]
+    zx_sends = [(ym, 7, 1, zp, 4), (yp, 7, 1, zp, 5), (y2, 7, 1, zp, 6)]
     y_sends = [(n, 0, 4, yp, 7), (n, 0, 4, ym, 8), (n, 4, 4, yp, 9), (n, 4, 4, ym, 10)]
     y_fwds = [(ym, 0, 2, yp, 11), (yp, 2, 2, ym, 12), (ym, 4, 2, yp, 13), (yp, 6, 2, ym, 14)]
-    p_sends = [(zp, 0, 4, yp, 15), (zp, 0, 4, ym, 16), (zp, 4, 2, yp, 17), (zp, 4, 2, ym, 18)]
-    p_fwds = [(zym, 0, 2, yp, 19), (zyp, 2, 2, ym, 20), (zym, 4, 1, yp, 21), (zyp, 5, 1, ym, 22)]
+    p_sends = [
+        (zp, 0, 2, yp, 15), (zp, 0, 2, ym, 16), (zp, 2, 2, yp, 17), (zp, 2, 2, ym, 18), (zp, 4, 2, yp, 19),
+        (zp, 4, 2, ym, 20), (zp, 6, 1, yp, 25), (zp, 6, 1, ym, 26),
+    ]
+    p_fwds = [(zym, 0, 2, yp, 21), (zyp, 2, 2, ym, 22), (zym, 4, 1, yp, 23), (zyp, 5, 1, ym, 24), (zym, 6, 1, yp, 27)]
     every = z_sends + zx_sends + y_sends + y_fwds + p_sends + p_fwds
 
     def go(messages):
@@ -126,8 +132,9 @@
         rtr[0, :, rows] = hi.T
         rtr[1, :, rows] = lo.T
 
-    part, xrecv, rsr = (part0, part1, part2), (xrecv0, xrecv1, xrecv2), (rsr0, rsr1, rsr2)
-    half_rows = (128, M0 // 2, M1 // 2)
+    part, xrecv = (part0, part1, part2, part3), (xrecv0, xrecv1, xrecv2, xrecv3)
+    rsr = (rsr0, rsr1, rsr2, rsr3)
+    half_rows = (128,) + tuple(m // 2 for m in PARTS)
     myrows = pl.ds(mult(c, 128), 128)
     hisrows = pl.ds(mult(1 - c, 128), 128)
 
@@ -160,16 +167,16 @@
             def _():
                 rs_copy(st, kk).start()
 
-    def reduce_start(st, compute, hooks=()):
+    def reduce_start(st, compute, hooks=(), lag=1):
         @pl.loop(0, 4)
         def _(s):
             i = order(s)
             part[st][:, pl.ds(mult(i, 256), 256)] = compute(i)
             x_copy(st, i).start()
 
-            @pl.when(s >= 1)
+            @pl.when(s >= lag)
             def _():
-                finish(st, order(s - 1))
+                finish(st, order(s - lag))
 
             for at, hook in hooks:
 
@@ -193,7 +200,11 @@
 
     def project(i):
         v_load(i).wait()
-        return dot3((rtr[0], rtr[1]), split(v[:, pl.ds(mult(i, 256), 256)]))
+        cols = pl.ds(mult(i, 256), 256)
+        hi, lo = split(v[:, cols])
+        uu[0, :, cols] = hi
+        uu[1, :, cols] = lo
+        return dot3((rtr[0], rtr[1]), (hi, lo))
 
     reduce_start(0, project)
 
@@ -219,14 +230,9 @@
     @pl.loop(0, 2)
     def _(i):
         rows = pl.ds(mult(i, 1024), 1024)
-        hi, lo = split(dot3(ttt, (rtr[0, :, rows], rtr[1, :, rows])))
-        rtt[0:256, rows] = hi
-        rtt[256:512, rows] = lo
-        rtt[512:768, rows] = hi
-
-    arrived(ym, 0, 4)
-    arrived(yp, 0, 4)
-    go(y_fwds[:2])
+        hi, lo = split(dot3(ttt, (rtr[0, :, rows], rtr[1, :, rows])) * ep[:, rows])
+        yt[0, :, rows] = hi
+        yt[1, :, rows] = lo
 
     x, zl = lax.rem(k, 4), k // 4
     kz = (1 - zl) * 4 + x
@@ -250,25 +256,42 @@
             pfull.at[myrows, cols], pfull.at[myrows, cols], pr_s.at[kk], pr_r.at[kk], partner
         )
 
-    total = reduce_end(0)
-    pfull[myrows, pl.ds(mult(k, 128), 128)] = total
-    for m in slices:
-        slice_copy(*m).start()
-    relay(k).start()
-    go(z_sends[2:])
-    arrived(ym, 4, 4)
-    arrived(yp, 4, 4)
-    go(y_fwds[2:])
+    def own_slice():
+        pfull[myrows, pl.ds(mult(k, 128), 128)] = reduce_end(0)
+        for m in slices:
+            slice_copy(*m).start()
+
+        relay(k).start()
+        go(z_sends[2:])
+
+    @pl.loop(0, 4)
+    def _(i):
+        cols = pl.ds(mult(i, 256), 256)
+        a3[:, cols] = dot3((yt[0], yt[1]), (uu[0, :, cols], uu[1, :, cols]))
+
+        @pl.when(i == 1)
+        def _():
+            arrived(ym, 0, 4)
+            arrived(yp, 0, 4)
+            go(y_fwds[:2])
+            own_slice()
+
+        @pl.when(i == 2)
+        def _():
+            arrived(ym, 4, 4)
+            arrived(yp, 4, 4)
+            go(y_fwds[2:])
+
     slice_here(kz)
     for m in z_slices:
         slice_copy(*m).start()
     relay(kz).start()
     arrived(zp, 0, 2)
-    arrived(zp, 2, 2)
     go(p_sends[:2])
     for kx in x_peers:
         slice_here(kx)
         relay(kx).start()
+
     def relay_in(kk):
         cols = pl.ds(mult(kk, 128), 128)
         return remote(pfull.at[hisrows, cols], pfull.at[hisrows, cols], pr_s.at[0], pr_r.at[kk], partner)
@@ -296,123 +319,164 @@
         for nn in peers:
             pb_copy(nn).start()
 
-    uu[0, ROWS:, :] = jnp.zeros((KP - ROWS, NC), BF16)
-    uu[1, ROWS:, :] = jnp.zeros((KP - ROWS, NC), BF16)
-
-    def update(zz):
-        @pl.loop(0, 2)
-        def _(j):
-            cols = pl.ds(mult(2 * zz + j, 256), 256)
-            p = split(pfull[:, cols])
-            u = v[:ROWS, cols] - dot3((rt[0, :ROWS, :], rt[1, :ROWS, :]), p)
-            u_out[:, cols] = u
-            hi, lo = split(u)
-            uu[0, :ROWS, cols] = hi
-            uu[1, :ROWS, cols] = lo
-
+    blocks = [base + d for d in range(4)] + [zp, zyp, zym, zy2]
+    firsts = (0, PARTS[0], PARTS[0] + PARTS[1])
+
+    def sources(h):
+        if h == 0:
+            return [pl.ds(mult(zh, 4 * BW), 4 * BW)]
+        return [pl.ds(mult(nn, BW), BW) for nn in (blocks[4:7] if h == 1 else blocks[7:])]
+
+    def scaled(h):
+        at, m = 0, PARTS[h]
+        for src in sources(h):
+            hi, lo = split(vbt[src, :] * ep[...])
+            ub[at : at + hi.shape[0], :] = hi
+            ub[m + at : m + at + hi.shape[0], :] = lo
+            at += hi.shape[0]
+
+    hi, lo = split(dot3((yt[0], yt[1]), (rt[0], rt[1])))
+    a4[0] = hi
+    a4[1] = lo
     for kx in [k] + x_peers:
         slice_arrived(kx)
 
-    @pl.when(zl == 0)
+    @pl.when((zl == 1) & (kz != KB))
     def _():
+        slice_here(KB)
+        relay(KB).start()
+
+    def block_columns():
+        @pl.when(zl == 1)
+        def _():
+            slice_arrived(KB)
+
         pb_send()
-
-    update(zl)
+        arrived(zp, 2, 2)
+        go(p_sends[2:4] + zx_sends[:2])
+        arrived(zp, 4, 2)
+        go(p_sends[4:6])
+
     z_peers = [(1 - zl) * 4 + lax.rem(x + d, 4) for d in (1, 3, 2)]
-    for kx in z_peers:
-        slice_here(kx)
-        relay(kx).start()
-    for kx in [kz] + z_peers:
-        slice_arrived(kx)
-
-    @pl.when(zl == 1)
-    def _():
-        pb_send()
-
-    arrived(zp, 4, 2)
-    go(p_sends[2:])
-    arrived(y2, 6, 2)
-    go(zx_sends)
-    update(1 - zl)
-    arrived(zym, 0, 4)
-    arrived(zyp, 0, 4)
-    go(p_fwds[:2])
-    for nn in peers:
-        pb_in(nn).wait_recv()
-        pb_relay(nn, c).start()
-    for nn in peers:
-        pb_relay(nn, 1 - c).wait_recv()
-
-    blocks = [base + d for d in range(4)] + [zp, zyp, zy2, zym]
-
-    def f_copy(h):
-        first = h * M0
-        rows = pl.ds(pl.multiple_of(first + c * half_rows[1 + h], 32), half_rows[1 + h])
-        return remote(fl.at[rows], fl.at[rows], f_s.at[h], f_r.at[h], partner)
-
-    def fock(h, hooks=()):
-        srcs = [pl.ds(mult(nn, BW), BW) for nn in (blocks[:5] if h == 0 else blocks[5:])]
-        if h == 0:
-            srcs = [pl.ds(mult(zh, 4 * BW), 4 * BW)] + srcs[4:]
-        hi, lo = split(jnp.concatenate([pbt[src, :] for src in srcs], axis=0))
-        p = jnp.concatenate([hi, hi, lo], axis=1)
-
-        @pl.loop(0, 2)
-        def _(i):
-            cols = pl.ds(mult(i, 1024), 1024)
-            vv = jnp.concatenate([vbt[src, cols] for src in srcs], axis=0)
-            hi, lo = split((vv - dot(p, rtt[:, cols])) * ep[:, cols])
-            ub[0, : hi.shape[0], cols] = hi
-            ub[1, : hi.shape[0], cols] = lo
-
-        m = M0 if h == 0 else M1
-
-        def compute(i):
-            cols = pl.ds(mult(i, 256), 256)
-            return dot3((ub[0, :m], ub[1, :m]), (uu[0, :, cols], uu[1, :, cols]))
-
-        reduce_start(1 + h, compute, hooks)
-
-    def fock_end(h):
-        first = h * M0
-        rows = pl.ds(pl.multiple_of(first + c * half_rows[1 + h], 32), half_rows[1 + h])
-        fl[rows, :] = reduce_end(1 + h)
-        f_copy(h).start()
-
-    for o in (0, 2, 4):
-        arrived(y2, o, 2)
-    arrived(zp, 6, 2)
+
+    def pb_pass(some):
+        for nn in some:
+            pb_in(nn).wait_recv()
+            pb_relay(nn, c).start()
+
+    def others():
+        for kx in z_peers:
+
+            @pl.when((zl == 0) | (kx != KB))
+            def _():
+                slice_here(kx)
+                relay(kx).start()
+
+        for o in (0, 2, 4, 6):
+            arrived(y2, o, 2)
+        go(zx_sends[2:])
+        scaled(0)
+        arrived(zp, 6, 2)
+        go(p_sends[6:])
+        arrived(zym, 0, 2)
+        go(p_fwds[:1])
+        for kx in [kz] + z_peers:
+
+            @pl.when((zl == 0) | (kx != KB))
+            def _():
+                slice_arrived(kx)
+
+    @pl.loop(0, 4)
+    def _(s):
+        cols = pl.ds(mult(lax.rem(2 * zl + s, 4), 256), 256)
+        p = split(pfull[:, cols])
+        u = v[:ROWS, cols] - dot3((rt[0, :ROWS, :], rt[1, :ROWS, :]), p)
+        u_out[:, cols] = u
+        hi, lo = split(u)
+        uu[0, :ROWS, cols] = hi
+        uu[1, :ROWS, cols] = lo
+        hi, lo = split(a3[:, cols] - dot3((a4[0], a4[1]), p))
+        bb[0, :, cols] = hi
+        bb[1, :, cols] = lo
+
+        @pl.when(s == 0)
+        def _():
+            block_columns()
+
+        @pl.when(s == 1)
+        def _():
+            others()
+
+        @pl.when(s == 2)
+        def _():
+            pb_pass(peers[:3])
+
+    def f_rows(h, cc):
+        rows = pl.ds(pl.multiple_of(firsts[h] + cc * half_rows[1 + h], 32), half_rows[1 + h])
+        return fl.at[rows]
+
+    def f_copy(h, cc):
+        return remote(f_rows(h, cc), f_rows(h, cc), f_s.at[h], f_r.at[h], partner)
+
+    def pb_part(h, i):
+        cols = pl.ds(mult(i, 256), 256)
+        return dot3(split(jnp.concatenate([pbt[src, :] for src in sources(h)], axis=0)), (bb[0, :, cols], bb[1, :, cols]))
+
+    def main_part(h, i):
+        m = PARTS[h]
+        cols = pl.ds(mult(i, 256), 256)
+        if h < 2:
+            return dot3((ub[:m], ub[m : 2 * m]), (uu[0, :, cols], uu[1, :, cols]))
+        both = dot(ub[: 2 * m], uu[0, :, cols])
+        return both[:m] + both[m:] + dot(ub[:m], uu[1, :, cols])
+
+    def pass_some():
+        arrived(zyp, 2, 2)
+        go(p_fwds[1:2])
+        pb_pass(peers[3:])
 
     def pass_last():
         arrived(zym, 4, 2)
         arrived(zyp, 4, 2)
-        go(p_fwds[2:])
-
-    fock(0, [(0, pass_last)])
-    arrived(zym, 6, 2)
-    arrived(zyp, 6, 2)
-    for o, cnt in ((0, 2), (2, 2), (4, 1), (5, 1), (6, 2)):
+        go(p_fwds[2:4])
+
+    def fock_end(h):
+        f_rows(h, c)[...] = reduce_end(1 + h)
+        f_copy(h, c).start()
+
+    for nn in peers[:3]:
+        pb_relay(nn, 1 - c).wait_recv()
+    reduce_start(1, lambda i: main_part(0, i) - pb_part(0, i), [(1, pass_some), (3, pass_last)])
+    arrived(zym, 6, 1)
+    go(p_fwds[4:])
+    for nn in peers[3:]:
+        pb_relay(nn, 1 - c).wait_recv()
+    for src, o, cnt in ((zym, 2, 2), (zym, 7, 1), (zyp, 0, 2), (zyp, 6, 1), (zyp, 7, 1)):
+        arrived(src, o, cnt)
+    scaled(1)
+    reduce_start(2, lambda i: main_part(1, i) - pb_part(1, i), [(0, lambda: finish(1, order(3)))])
+    finish(2, order(3))
+    for o, cnt in ((0, 2), (2, 2), (4, 1), (5, 1), (6, 1), (7, 1)):
         arrived(zy2, o, cnt)
-    fock(1, [(0, lambda: finish(1, order(3)))])
-    finish(2, order(3))
+    scaled(2)
+    reduce_start(3, lambda i: main_part(2, i) - pb_part(2, i), lag=2)
+    finish(3, order(2))
+    finish(3, order(3))
     fock_end(0)
     fock_end(1)
-    def f_in(h):
-        rows = pl.ds(pl.multiple_of(h * M0 + (1 - c) * half_rows[1 + h], 32), half_rows[1 + h])
-        return remote(fl.at[rows], fl.at[rows], f_s.at[h], f_r.at[h], partner)
-
-    for h in range(2):
-        f_in(h).wait_recv()
+    fock_end(2)
+    for h in range(3):
+        f_copy(h, 1 - c).wait_recv()
     for at, nn in enumerate(blocks):
         fg[pl.ds(mult(nn, BW), BW), :] = fl[at * BW : (at + 1) * BW, :]
     ft[...] = fg[...].T
     f_out[...] = ft[pl.ds(mult(c, BW), BW), :]
 
-    for h in range(2):
-        f_copy(h).wait_send()
+    for h in range(3):
+        f_copy(h, c).wait_send()
     for m in every:
         ag(*m).wait_send()
-    for st in range(3):
+    for st in range(4):
         reduce_drain(st)
     for m in slices + z_slices:
         slice_copy(*m).wait_send()
@@ -443,28 +507,25 @@
             pltpu.VMEM((1, ROWS), F32),
             pltpu.VMEM((2, NB, KP), BF16),
             pltpu.VMEM((2, KP, NB), BF16),
-            pltpu.VMEM((3 * NB, KP), BF16),
+            pltpu.VMEM((2, NB, KP), BF16),
+            pltpu.VMEM((NB, NC), F32),
+            pltpu.VMEM((2, NB, NB), BF16),
+            pltpu.VMEM((2, NB, NC), BF16),
             pltpu.VMEM((2, KP, NC), BF16),
             pltpu.VMEM((FB, KP), F32),
             pltpu.VMEM((FB, NB), F32),
             pltpu.VMEM((1, KP), F32),
+            *[pltpu.VMEM((m, NC), F32) for m in (NB,) + PARTS],
+            *[pltpu.VMEM((m // 2, NC), F32) for m in (NB,) + PARTS],
+            *[pltpu.VMEM((8, m // 2, 128), F32) for m in (NB,) + PARTS],
             pltpu.VMEM((NB, NC), F32),
-            pltpu.VMEM((M0, NC), F32),
-            pltpu.VMEM((M1, NC), F32),
-            pltpu.VMEM((128, NC), F32),
-            pltpu.VMEM((M0 // 2, NC), F32),
-            pltpu.VMEM((M1 // 2, NC), F32),
-            pltpu.VMEM((8, 128, 128), F32),
-            pltpu.VMEM((8, M0 // 2, 128), F32),
-            pltpu.VMEM((8, M1 // 2, 128), F32),
-            pltpu.VMEM((NB, NC), F32),
-            pltpu.VMEM((2, M0, KP), BF16),
+            pltpu.VMEM((2 * PARTS[0], KP), BF16),
             pltpu.VMEM((FB, 128), F32),
             pltpu.VMEM((FB, 128), F32),
             pltpu.VMEM((128, FB), F32),
-            dma((8,)), dma((23,)), dma((64,)), dma((12,)), dma((12,)),
-            dma((24,)), dma((24,)), dma((8,)), dma((8,)), dma((8,)), dma((8,)),
-            dma((16,)), dma((16,)), dma((2,)), dma((2,)),
+            dma((8,)), dma((28,)), dma((64,)), dma((16,)), dma((16,)),
+            dma((32,)), dma((32,)), dma((7,)), dma((8,)), dma((8,)), dma((8,)),
+            dma((16,)), dma((16,)), dma((3,)), dma((3,)),
         ],
         compiler_params=pltpu.CompilerParams(
             collective_id=0, has_side_effects=True, vmem_limit_bytes=50 * 2**20

time: 65.6 us -> 62.1 us (0.947)
  Pallas kernels: 60.8 us -> 57.4 us
    pallas_call x1, Pallas kernels: 60.8 us -> 57.4 us  [on_device(): pl.pallas_call(kernel, out_shape=(pltpu.VMEM((ROWS, NC), F32), pltpu.VMEM...]
where the time goes in v3:
time: 62.1 us; the launch traced here: 62 us
  Pallas kernels  57.4 us (92%)
  local copies, waits for them, and re-layouts  3.99 us (6%)
  between operations  0.64 us (1%)
    pallas_call x1, Pallas kernels, on_device(): pl.pallas_call(kernel, out_shape=(pltpu.VMEM((ROWS, NC), F32), pltpu.VMEM...  57.4 us
    unnamed x2, local copies, waits for them, and re-layouts  3.99 us

profile of v3, /device:TPU:1, one launch (start us, length us, event | category | flops | bytes accessed | tf_op | source)
XLA Modules:
  0.0 62.0 jit_solution(9647965521440205525)
XLA Ops:
  0.6 57.4 %reflect_fock.1 = (f32[2000,1024]{1,0:T(8,128)S(1)}, f32[64,512]{1,0:T(8,128)S(1)}) custom-call(f32[2000,1024]{1,0:T(8,128)} %v_hbm.1, f32[2000,256]{1,0:T(8,128)} %r_hbm.1, f32[256,256]{1,0:T(8,128)} %t_hbm.1, f32[1,2000]{1,0:T(1,128)} %bitcast.1), custom_call_target="tpu_custom_call" | custom-call | tf_op jit(solution)/shard_map/reflect_fock/pallas_call | solution.py:494
  58.0 3.3 %copy.8 = f32[2000,1024]{1,0:T(8,128)} copy(f32[2000,1024]{1,0:T(8,128)S(1)} %get-tuple-element.2) | data formatting | bytes 16384000
  61.4 0.7 %copy.9 = f32[64,512]{1,0:T(8,128)} copy(f32[64,512]{1,0:T(8,128)S(1)} %get-tuple-element.3) | data formatting | bytes 262144

commit v4 on v3

--- a/solution.py
+++ b/solution.py
@@ -35,7 +35,7 @@
 def kernel(
     v_hbm, r_hbm, t_hbm, e_hbm, u_out, f_out,
     v, r, vb, t_ref, e_ref, rtr, rt, yt, a3, a4, bb, uu, vbt, pbt, ep, part0, part1, part2, part3, xrecv0, xrecv1, xrecv2,
-    xrecv3, rsr0, rsr1, rsr2, rsr3, pfull, ub, fl, fg, ft,
+    rsr0, rsr1, rsr2, rsr3, pfull, ub, fl, fx,
     ld_sem, ag_s, ag_r, xs, xr, rs_s, rs_r, pa_s, pa_r, pr_s, pr_r, pb_s, pb_r, f_s, f_r,
 ):
     w, n = lax.axis_index("wide"), lax.axis_index("narrow")
@@ -132,14 +132,14 @@
         rtr[0, :, rows] = hi.T
         rtr[1, :, rows] = lo.T
 
-    part, xrecv = (part0, part1, part2, part3), (xrecv0, xrecv1, xrecv2, xrecv3)
+    part, xrecv = (part0, part1, part2, part3), (xrecv0, xrecv1, xrecv2)
     rsr = (rsr0, rsr1, rsr2, rsr3)
-    half_rows = (128,) + tuple(m // 2 for m in PARTS)
+    half_rows = (128, PARTS[0] // 2, PARTS[1] // 2, PARTS[2])
     myrows = pl.ds(mult(c, 128), 128)
     hisrows = pl.ds(mult(1 - c, 128), 128)
 
     def mine(st):
-        return pl.ds(mult(c, half_rows[st]), half_rows[st])
+        return pl.ds(mult(c if st < 3 else 0, half_rows[st]), half_rows[st])
 
     def his(st):
         return pl.ds(mult(1 - c, half_rows[st]), half_rows[st])
@@ -156,10 +156,7 @@
             rs_r.at[st * 8 + k], same_core(kk),
         )
 
-    def finish(st, i):
-        cols = pl.ds(mult(i, 256), 256)
-        x_copy(st, i).wait_recv()
-        part[st][mine(st), cols] = part[st][mine(st), cols] + xrecv[st][:, cols]
+    def scatter(st, i):
         for t in range(2):
             kk = 2 * i + t
 
@@ -167,16 +164,22 @@
             def _():
                 rs_copy(st, kk).start()
 
-    def reduce_start(st, compute, hooks=(), lag=1):
+    def finish(st, i):
+        cols = pl.ds(mult(i, 256), 256)
+        x_copy(st, i).wait_recv()
+        part[st][mine(st), cols] = part[st][mine(st), cols] + xrecv[st][:, cols]
+        scatter(st, i)
+
+    def reduce_start(st, compute, hooks=()):
         @pl.loop(0, 4)
         def _(s):
             i = order(s)
             part[st][:, pl.ds(mult(i, 256), 256)] = compute(i)
             x_copy(st, i).start()
 
-            @pl.when(s >= lag)
+            @pl.when(s >= 1)
             def _():
-                finish(st, order(s - lag))
+                finish(st, order(s - 1))
 
             for at, hook in hooks:
 
@@ -193,7 +196,7 @@
         return total
 
     def reduce_drain(st):
-        for i in range(4):
+        for i in range(4 if st < 3 else 0):
             x_copy(st, i).wait_send()
         for d in range(1, 8):
             rs_copy(st, lax.rem(k + d, 8)).wait_send()
@@ -282,6 +285,9 @@
             arrived(yp, 4, 4)
             go(y_fwds[2:])
 
+    hi, lo = split(dot3((yt[0], yt[1]), (rt[0], rt[1])))
+    a4[0] = hi
+    a4[1] = lo
     slice_here(kz)
     for m in z_slices:
         slice_copy(*m).start()
@@ -335,9 +341,6 @@
             ub[m + at : m + at + hi.shape[0], :] = lo
             at += hi.shape[0]
 
-    hi, lo = split(dot3((yt[0], yt[1]), (rt[0], rt[1])))
-    a4[0] = hi
-    a4[1] = lo
     for kx in [k] + x_peers:
         slice_arrived(kx)
 
@@ -412,11 +415,11 @@
             pb_pass(peers[:3])
 
     def f_rows(h, cc):
-        rows = pl.ds(pl.multiple_of(firsts[h] + cc * half_rows[1 + h], 32), half_rows[1 + h])
-        return fl.at[rows]
+        first = firsts[h] + cc * half_rows[1 + h] if h < 2 else firsts[2]
+        return fl.at[pl.ds(pl.multiple_of(first, 32), half_rows[1 + h])]
 
     def f_copy(h, cc):
-        return remote(f_rows(h, cc), f_rows(h, cc), f_s.at[h], f_r.at[h], partner)
+        return remote(f_rows(h, cc), f_rows(h, cc) if h < 2 else fx, f_s.at[h], f_r.at[h], partner)
 
     def pb_part(h, i):
         cols = pl.ds(mult(i, 256), 256)
@@ -455,22 +458,27 @@
         arrived(src, o, cnt)
     scaled(1)
     reduce_start(2, lambda i: main_part(1, i) - pb_part(1, i), [(0, lambda: finish(1, order(3)))])
-    finish(2, order(3))
     for o, cnt in ((0, 2), (2, 2), (4, 1), (5, 1), (6, 1), (7, 1)):
         arrived(zy2, o, cnt)
     scaled(2)
-    reduce_start(3, lambda i: main_part(2, i) - pb_part(2, i), lag=2)
-    finish(3, order(2))
-    finish(3, order(3))
+    @pl.loop(0, 4)
+    def _(s):
+        i = order(s)
+        part3[:, pl.ds(mult(i, 256), 256)] = main_part(2, i) - pb_part(2, i)
+
+        @pl.when(s == 0)
+        def _():
+            finish(2, order(3))
+
+        scatter(3, i)
+
     fock_end(0)
     fock_end(1)
     fock_end(2)
     for h in range(3):
         f_copy(h, 1 - c).wait_recv()
-    for at, nn in enumerate(blocks):
-        fg[pl.ds(mult(nn, BW), BW), :] = fl[at * BW : (at + 1) * BW, :]
-    ft[...] = fg[...].T
-    f_out[...] = ft[pl.ds(mult(c, BW), BW), :]
+    f_out[: firsts[2], :] = fl[: firsts[2], :]
+    f_out[firsts[2] :, :] = fl[firsts[2] :, :] + fx[...]
 
     for h in range(3):
         f_copy(h, c).wait_send()
@@ -487,15 +495,35 @@
         relay(kk).wait_send()
 
 
+def store(u, f, u_hbm, f_hbm, fg, ft, fo, sem):
+    copies = []
+    for i in range(10):
+        rows = pl.ds(200 * i, 200)
+        copies.append(pltpu.make_async_copy(u.at[rows], u_hbm.at[rows], sem.at[i]))
+    for copy in copies:
+        copy.start()
+    c, n = lax.rem(lax.axis_index("wide"), 2), lax.axis_index("narrow")
+    y, base, zbase = lax.rem(n, 4), n // 4 * 4, (1 - n // 4) * 4
+    zp, zyp, zym, zy2 = [zbase + lax.rem(y + d, 4) for d in (0, 1, 3, 2)]
+    for at, nn in enumerate([base + d for d in range(4)] + [zp, zyp, zym, zy2]):
+        fg[pl.ds(mult(nn, BW), BW), :] = f[at * BW : (at + 1) * BW, :]
+    ft[...] = fg[...].T
+    fo[...] = ft[pl.ds(mult(c, BW), BW), :]
+    copies.append(pltpu.make_async_copy(fo, f_hbm, sem.at[10]))
+    copies[-1].start()
+    for copy in copies:
+        copy.wait()
+
+
 def on_device(vectors, reflectors, triangle, energies):
     vm = pl.BlockSpec(memory_space=pltpu.VMEM)
     hbm = pl.BlockSpec(memory_space=pl.ANY)
     dma = pltpu.SemaphoreType.DMA
-    return pl.pallas_call(
+    u, f = pl.pallas_call(
         kernel,
         out_shape=(
             pltpu.VMEM((ROWS, NC), F32),
-            pltpu.VMEM((BW, FB), F32),
+            pltpu.VMEM((FB, 128), F32),
         ),
         in_specs=[hbm, hbm, hbm, hbm],
         out_specs=(vm, vm),
@@ -516,13 +544,13 @@
             pltpu.VMEM((FB, NB), F32),
             pltpu.VMEM((1, KP), F32),
             *[pltpu.VMEM((m, NC), F32) for m in (NB,) + PARTS],
-            *[pltpu.VMEM((m // 2, NC), F32) for m in (NB,) + PARTS],
-            *[pltpu.VMEM((8, m // 2, 128), F32) for m in (NB,) + PARTS],
+            *[pltpu.VMEM((m // 2, NC), F32) for m in (NB,) + PARTS[:2]],
+            *[pltpu.VMEM((8, m // 2, 128), F32) for m in (NB,) + PARTS[:2]],
+            pltpu.VMEM((8, PARTS[2], 128), F32),
             pltpu.VMEM((NB, NC), F32),
             pltpu.VMEM((2 * PARTS[0], KP), BF16),
             pltpu.VMEM((FB, 128), F32),
-            pltpu.VMEM((FB, 128), F32),
-            pltpu.VMEM((128, FB), F32),
+            pltpu.VMEM((PARTS[2], 128), F32),
             dma((8,)), dma((28,)), dma((64,)), dma((16,)), dma((16,)),
             dma((32,)), dma((32,)), dma((7,)), dma((8,)), dma((8,)), dma((8,)),
             dma((16,)), dma((16,)), dma((3,)), dma((3,)),
@@ -532,6 +560,23 @@
         ),
         name="reflect_fock",
     )(vectors, reflectors, triangle, energies[None, :])
+    return pl.pallas_call(
+        store,
+        out_shape=(
+            jax.ShapeDtypeStruct((ROWS, NC), F32),
+            jax.ShapeDtypeStruct((BW, FB), F32),
+        ),
+        in_specs=[vm, vm],
+        out_specs=(hbm, hbm),
+        scratch_shapes=[
+            pltpu.VMEM((FB, 128), F32),
+            pltpu.VMEM((128, FB), F32),
+            pltpu.VMEM((BW, FB), F32),
+            dma((11,)),
+        ],
+        compiler_params=pltpu.CompilerParams(vmem_limit_bytes=2**21),
+        name="store",
+    )(u, f)
 
 
 def solution(mesh):

time: 62.1 us -> 60.8 us (0.979)
  local copies, waits for them, and re-layouts: 3.99 us -> 0 us
  Pallas kernels: 57.4 us -> 60 us
    unnamed x2 -> x0, local copies, waits for them, and re-layouts: 3.99 us -> none
    pallas_call x0 -> x1, Pallas kernels: none -> 3.38 us  [on_device(): pl.pallas_call(store, out_shape=(jax.ShapeDtypeStruct((ROWS, NC), F32), j...]
    pallas_call x1, Pallas kernels: 57.4 us -> 56.7 us  [on_device(): pl.pallas_call(kernel, out_shape=(pltpu.VMEM((ROWS, NC), F32), pltpu.VMEM...]
where the time goes in v4:
time: 60.8 us; the launch traced here: 60.7 us
  Pallas kernels  60 us (99%)
  between operations  0.64 us (1%)
    pallas_call x1, Pallas kernels, on_device(): pl.pallas_call(kernel, out_shape=(pltpu.VMEM((ROWS, NC), F32), pltpu.VMEM...  56.7 us
    pallas_call x1, Pallas kernels, on_device(): pl.pallas_call(store, out_shape=(jax.ShapeDtypeStruct((ROWS, NC), F32), j...  3.38 us

profile of v4, /device:TPU:1, one launch (start us, length us, event | category | flops | bytes accessed | tf_op | source)
XLA Modules:
  0.0 60.7 jit_solution(940205594636440461)
XLA Ops:
  0.6 56.7 %reflect_fock.1 = (f32[2000,1024]{1,0:T(8,128)S(1)}, f32[512,128]{1,0:T(8,128)S(1)}) custom-call(f32[2000,1024]{1,0:T(8,128)} %v_hbm.1, f32[2000,256]{1,0:T(8,128)} %r_hbm.1, f32[256,256]{1,0:T(8,128)} %t_hbm.1, f32[1,2000]{1,0:T(1,128)} %bitcast.1), custom_call_target="tpu_custom_call" | custom-call | tf_op jit(solution)/shard_map/reflect_fock/pallas_call | solution.py:522
  57.3 3.4 %store.1 = (f32[2000,1024]{1,0:T(8,128)}, f32[64,512]{1,0:T(8,128)}) custom-call(f32[2000,1024]{1,0:T(8,128)S(1)} %get-tuple-element.4.u, f32[512,128]{1,0:T(8,128)S(1)} %get-tuple-element.5.f), custom_call_target="tpu_custom_call" | custom-call | tf_op jit(solution)/shard_map/store/pallas_call | solution.py:563

commit v5 on v4

--- a/solution.py
+++ b/solution.py
@@ -450,6 +450,7 @@
     for nn in peers[:3]:
         pb_relay(nn, 1 - c).wait_recv()
     reduce_start(1, lambda i: main_part(0, i) - pb_part(0, i), [(1, pass_some), (3, pass_last)])
+    finish(1, order(3))
     arrived(zym, 6, 1)
     go(p_fwds[4:])
     for nn in peers[3:]:
@@ -457,22 +458,19 @@
     for src, o, cnt in ((zym, 2, 2), (zym, 7, 1), (zyp, 0, 2), (zyp, 6, 1), (zyp, 7, 1)):
         arrived(src, o, cnt)
     scaled(1)
-    reduce_start(2, lambda i: main_part(1, i) - pb_part(1, i), [(0, lambda: finish(1, order(3)))])
+    reduce_start(2, lambda i: main_part(1, i) - pb_part(1, i))
+    finish(2, order(3))
     for o, cnt in ((0, 2), (2, 2), (4, 1), (5, 1), (6, 1), (7, 1)):
         arrived(zy2, o, cnt)
+    fock_end(0)
     scaled(2)
     @pl.loop(0, 4)
     def _(s):
         i = order(s)
         part3[:, pl.ds(mult(i, 256), 256)] = main_part(2, i) - pb_part(2, i)
 
-        @pl.when(s == 0)
-        def _():
-            finish(2, order(3))
-
         scatter(3, i)
 
-    fock_end(0)
     fock_end(1)
     fock_end(2)
     for h in range(3):

time: 60.8 us -> 60.7 us (level)
  no operation moved by 1% of the time
where the time goes in v5:
time: 60.7 us; the launch traced here: 60.6 us
  Pallas kernels  60 us (99%)
  between operations  0.64 us (1%)
    pallas_call x1, Pallas kernels, on_device(): pl.pallas_call(kernel, out_shape=(pltpu.VMEM((ROWS, NC), F32), pltpu.VMEM...  56.6 us
    pallas_call x1, Pallas kernels, on_device(): pl.pallas_call(store, out_shape=(jax.ShapeDtypeStruct((ROWS, NC), F32), j...  3.38 us

profile of v5, /device:TPU:1, one launch (start us, length us, event | category | flops | bytes accessed | tf_op | source)
XLA Modules:
  0.0 60.6 jit_solution(11853554294190707550)
XLA Ops:
  0.6 56.6 %reflect_fock.1 = (f32[2000,1024]{1,0:T(8,128)S(1)}, f32[512,128]{1,0:T(8,128)S(1)}) custom-call(f32[2000,1024]{1,0:T(8,128)} %v_hbm.1, f32[2000,256]{1,0:T(8,128)} %r_hbm.1, f32[256,256]{1,0:T(8,128)} %t_hbm.1, f32[1,2000]{1,0:T(1,128)} %bitcast.1), custom_call_target="tpu_custom_call" | custom-call | tf_op jit(solution)/shard_map/reflect_fock/pallas_call | solution.py:520
  57.2 3.4 %store.1 = (f32[2000,1024]{1,0:T(8,128)}, f32[64,512]{1,0:T(8,128)}) custom-call(f32[2000,1024]{1,0:T(8,128)S(1)} %get-tuple-element.4.u, f32[512,128]{1,0:T(8,128)S(1)} %get-tuple-element.5.f), custom_call_target="tpu_custom_call" | custom-call | tf_op jit(solution)/shard_map/store/pallas_call | solution.py:561
